TPU v7x, 512 devices: a whole 4x4x16 slice. The times are simulated.
512 devices in a mesh: row: 32 (over y, z_hi, core), col: 16 (over z_lo, x).
Axes of the slice: x: 4, y: 4, z: 16 (z_hi: 4, z_lo: 4; z = z_hi * 4 + z_lo), core: 2. Of those that a mesh axis runs over, the one named last changes fastest.
Arguments:
- forcing_terms: float32 [32, 16, 2, 32, 128], P('row', 'col'), may hold values from -6 to 6
- diagonal_reciprocal: float32 [32, 16, 2, 128, 128], P('row', 'col'), may hold values from -0.5 to 0.5
- stiffness_submatrix: float32 [32, 16, 32, 128, 128], P('row', 'col'), may hold values from -0.1875 to 0.1875
- stiffness_source_index: int32 [32, 16, 32], P('row', 'col'), may hold values from 0 to 31
- stiffness_target_index: int32 [32, 16, 32], P('row', 'col'), may hold values from 0 to 63
- stiffness_nonzero_tally: int32 [32, 16], P('row', 'col'), may hold values from 1 to 32, as said below
- interpolant_submatrix: float32 [32, 16, 16, 128, 128], P('row', 'col'), may hold values from -0.0625 to 0.0625
- interpolant_cluster_index: int32 [32, 16, 16], P('row', 'col'), may hold values from 0 to 1
- interpolant_target_index: int32 [32, 16, 16], P('row', 'col'), may hold values from 0 to 63
- interpolant_nonzero_tally: int32 [32, 16], P('row', 'col'), may hold values from 1 to 16, as said below
- provisional_interpolant: float32 [32, 16, 2, 128], P('row', 'col'), may hold values from 0.2 to 1
- cluster_label: int32 [32, 16, 2, 128], P('row', 'col'), may hold values from 0 to 255
Outputs:
- relaxed_iterate: float32 [32, 16, 2, 32, 128], P('row', 'col')
- residual: float32 [32, 16, 2, 32, 128], P('row', 'col')
- coarse: float32 [32, 2, 32, 128], P('row')
Inputs may be any that keep to these rules, and one draw needn't show every extreme that they name: `stiffness_nonzero_tally`: tile slots at or past the count are unused; some pair has all 32 slots live in every draw. `interpolant_nonzero_tally`: tile slots at or past the count are unused; some pair has all 16 slots live in every draw.
All inputs are finite; a program needn't handle non-finite values.
Results may differ from a plain program's by a relative error of at most 0.0003.
Values sent between devices are 32-bit elements; how exact they have to be, the bound alone decides.
No kernel may reach another device: no remote copies, remote signals or barrier semaphores. Data moves between devices by JAX's collectives and lax.ppermute only.
A program may use at most 64 MiB of HBM per device.

v0:
```python
import jax
import jax.numpy as jnp
from jax import lax
from jax.sharding import PartitionSpec as P

omega = 0.7
highest = lax.Precision.HIGHEST
tile_group = 8


def loop_tiles(blocks, stiffness_submatrices, rows, cols, low, high, nout):
    nrhs = blocks.shape[1]
    width = blocks.shape[2]

    def add_group(index, total):
        start = index * tile_group
        piece = lax.dynamic_slice_in_dim(stiffness_submatrices, start, tile_group, 0)
        row_ids = lax.dynamic_slice_in_dim(rows, start, tile_group, 0)
        col_ids = lax.dynamic_slice_in_dim(cols, start, tile_group, 0)
        slots = start + jnp.arange(tile_group)
        live = ((slots >= low) & (slots < high)).astype(jnp.float32)
        inputs = jnp.take(blocks, col_ids, axis=0)
        product = jnp.einsum("ska,sab->skb", inputs, piece, precision=highest)
        onehot = (row_ids[:, None] == jnp.arange(nout)[None, :]).astype(jnp.float32) * live[:, None]
        return total + jnp.einsum("so,skb->okb", onehot, product, precision=highest)

    starting_guess = low // tile_group
    last = (high + tile_group - 1) // tile_group
    empty = jnp.zeros((nout, nrhs, width), jnp.float32)
    return lax.fori_loop(starting_guess, last, add_group, empty)


def gather_columns(vec):
    whole = lax.all_gather(vec[None, None], "row", axis=0, tiled=True)
    return whole.reshape(-1, vec.shape[1], vec.shape[2])


def precondition(vec, inverse):
    return jnp.einsum("pka,pab->pkb", vec, inverse, precision=highest)


def stiffness_product(vec, stiffness_submatrices, rows, cols, count):
    blocks = gather_columns(vec)
    ncol = lax.axis_size("col")
    pblocks = vec.shape[0]
    nout = ncol * pblocks
    partial_value = loop_tiles(blocks, stiffness_submatrices, rows, cols, jnp.int32(0), count, nout)
    partial_value = partial_value.reshape(1, ncol, pblocks, vec.shape[1], vec.shape[2])
    summed = lax.psum_scatter(partial_value, "col", scatter_dimension=1, tiled=True)
    return summed[0, 0]


def body(
    forcing_terms,
    diagonal_reciprocal,
    stiffness_submatrix,
    stiffness_source_index,
    stiffness_target_index,
    stiffness_nonzero_tally,
    interpolant_submatrix,
    interpolant_cluster_index,
    interpolant_target_index,
    interpolant_nonzero_tally,
    provisional_interpolant,
    cluster_label,
):
    source = forcing_terms[0, 0]
    inverse = diagonal_reciprocal[0, 0]
    stiffness_submatrices = stiffness_submatrix[0, 0]
    rows = stiffness_source_index[0, 0]
    cols = stiffness_target_index[0, 0]
    count = stiffness_nonzero_tally[0, 0]
    starting_guess = omega * precondition(source, inverse)
    image_field = stiffness_product(starting_guess, stiffness_submatrices, rows, cols, count)
    relaxed_iterate = starting_guess + omega * precondition(source - image_field, inverse)
    image_field = stiffness_product(relaxed_iterate, stiffness_submatrices, rows, cols, count)
    residual = source - image_field
    pblocks, nrhs, width = residual.shape
    blocks = gather_columns(residual)
    part = loop_tiles(
        blocks,
        interpolant_submatrix[0, 0],
        interpolant_cluster_index[0, 0],
        interpolant_target_index[0, 0],
        jnp.int32(0),
        interpolant_nonzero_tally[0, 0],
        pblocks,
    )
    weighted = (
        (residual * provisional_interpolant[0, 0][:, None, :])
        .transpose(1, 0, 2)
        .reshape(nrhs, pblocks * width)
    )
    onehot = (
        cluster_label[0, 0].reshape(-1)[:, None] == jnp.arange(pblocks * width)[None, :]
    ).astype(jnp.float32)
    tentative = jnp.dot(weighted, onehot, precision=highest)
    part = part + tentative.reshape(nrhs, pblocks, width).transpose(1, 0, 2)
    coarse = lax.psum(part, "col")
    return (relaxed_iterate[None, None], residual[None, None], coarse[None])


def solution(mesh):
    placed = (
        P("row", "col", None, None, None),
        P("row", "col", None, None, None),
        P("row", "col", None, None, None),
        P("row", "col", None),
        P("row", "col", None),
        P("row", "col"),
        P("row", "col", None, None, None),
        P("row", "col", None),
        P("row", "col", None),
        P("row", "col"),
        P("row", "col", None, None),
        P("row", "col", None, None),
    )
    return jax.shard_map(
        body,
        mesh=mesh,
        in_specs=placed,
        out_specs=(
            P("row", "col", None, None, None),
            P("row", "col", None, None, None),
            P("row", None, None, None),
        ),
        check_vma=False,
    )
```

profile of v0, /device:TPU:8, one launch (start us, length us, event | category | flops | bytes accessed | tf_op | source)
XLA Modules:
  0.0 539.8 jit_solution(16684769150870673594)
XLA Ops:
  7.2 0.0 copy-start
  7.2 0.0 all-gather.8.cloned.1.call-start
  7.2 0.8 copy-done
  8.1 1.6 convolution_multiply_fusion.1
  9.7 0.0 all-gather.8.cloned.1.call-update
  9.7 0.0 reduce-scatter.3.cloned.1.call-start
  10.4 76.2 %all-gather.8.cloned.1.call-done = f32[64,32,128]{2,1,0:T(8,128)} async-done(((f32[2,32,128]{2,1,0:T(8,128)}), f32[64,32,128]{2,1,0:T(8,128)}) %all-gather.8.cloned.1.call-update) | async-done | bytes 1048592 | tf_op jit(solution)/shard_map/all_gather | solution.py:34
  86.7 0.0 copy-start.3
  86.7 19.1 %while.30 = (s32[]{:T(128)}, f32[32,32,128]{2,0,1:T(8,128)S(1)}, s32[]{:T(128)}, s32[32]{0:T(128)}, s32[]{:T(128)}, /*index=5*/s32[32]{0:T(128)}, f32[64,32,128]...) while((s32[]{:T(128)}, f32[32,32,128]{2,0,1:T(8,128)S(1)}, ...), condition=%wide.region_1.3_spmd, body=%wide.region_0.2_spmd.sunk | while | flops 63080028 | bytes 2232807 | solution.py:30
  86.7 1.4 compare_and_fusion.6
  88.1 1.8 gather_fusion
  89.9 1.7 fusion.75
  91.6 0.7 dynamic_slice.46
  92.3 0.8 convolution_add_fusion.6
  93.1 1.4 compare_and_fusion.6
  94.5 1.8 gather_fusion
  96.3 1.7 fusion.75
  97.9 0.7 dynamic_slice.46
  98.7 0.8 convolution_add_fusion.6
  99.5 1.4 compare_and_fusion.6
  100.9 1.8 gather_fusion
  102.7 1.7 fusion.75
  104.3 0.7 dynamic_slice.46
  105.0 0.8 convolution_add_fusion.6
  105.9 1.1 copy.25
  107.0 0.0 reduce-scatter.3.cloned.1.call-update
  107.0 0.0 all-gather.10.cloned.1.call-start
  107.1 91.7 %reduce-scatter.3.cloned.1.call-done = f32[1,1,2,32,128]{4,3,2,1,0:T(8,128)} async-done(((f32[1,16,2,32,128]{4,3,2,1,0:T(8,128)}), f32[1,1,2,32,128]{4,3,2,1,0:T(8,128)}) %reduce-scatter.3.cloned.1.call-update) | async-done | bytes 32784 | tf_op jit(solution)/shard_map/reduce_scatter | solution.py:49
  198.8 1.6 fusion.45
  200.4 0.0 all-gather.10.cloned.1.call-update
  200.4 0.0 reduce-scatter.5.cloned.1.call-start
  200.5 68.7 %all-gather.10.cloned.1.call-done = f32[64,32,128]{2,1,0:T(8,128)} async-done(((f32[2,32,128]{2,1,0:T(8,128)}), f32[64,32,128]{2,1,0:T(8,128)}) %all-gather.10.cloned.1.call-update) | async-done | bytes 1048592 | tf_op jit(solution)/shard_map/all_gather | solution.py:34
  269.3 15.3 %while.31 = (s32[]{:T(128)}, f32[32,32,128]{2,0,1:T(8,128)S(1)}, s32[]{:T(128)}, s32[32]{0:T(128)S(1)}, s32[]{:T(128)}, /*index=5*/s32[32]{0:T(128)S(1)}, f32[64...) while((s32[]{:T(128)}, f32[32,32,128]{2,0,1:T(8,128)S(1)}, ...), condition=%wide.region_4.6_spmd, body=%wide.region_3.5_spmd.sunk | while | flops 63080028 | bytes 2232807 | solution.py:30
  269.3 0.8 compare_and_fusion.7
  270.2 1.8 gather_fusion.1
  271.9 1.7 fusion.80
  273.6 0.1 dynamic_slice.48
  273.7 0.8 convolution_add_fusion.7
  274.5 0.7 compare_and_fusion.7
  275.2 1.8 gather_fusion.1
  277.0 1.7 fusion.80
  278.7 0.1 dynamic_slice.48
  278.7 0.8 convolution_add_fusion.7
  279.6 0.7 compare_and_fusion.7
  280.3 1.8 gather_fusion.1
  282.1 1.7 fusion.80
  283.7 0.1 dynamic_slice.48
  283.8 0.8 convolution_add_fusion.7
  284.6 1.1 copy.26
  285.7 0.0 reduce-scatter.5.cloned.1.call-update
  285.8 0.0 all-gather.6.cloned.1.call-start
  285.8 90.4 %reduce-scatter.5.cloned.1.call-done = f32[1,1,2,32,128]{4,3,2,1,0:T(8,128)} async-done(((f32[1,16,2,32,128]{4,3,2,1,0:T(8,128)}), f32[1,1,2,32,128]{4,3,2,1,0:T(8,128)}) %reduce-scatter.5.cloned.1.call-update) | async-done | bytes 32784 | tf_op jit(solution)/shard_map/reduce_scatter | solution.py:49
  376.2 1.4 sub.30
  377.6 0.0 all-gather.6.cloned.1.call-update
  378.3 0.8 fusion.52
  379.2 67.5 %all-gather.6.cloned.1.call-done = f32[32,1,2,32,128]{4,3,2,1,0:T(8,128)} async-done(((f32[1,1,2,32,128]{4,3,2,1,0:T(8,128)}), f32[32,1,2,32,128]{4,3,2,1,0:T(8,128)}) %all-gather.6.cloned.1.call-update) | async-done | bytes 1048592 | tf_op jit(solution)/shard_map/all_gather | solution.py:34
  446.8 3.6 while.32
  446.8 0.7 compare_and_fusion.8
  447.5 1.8 gather_fusion.2
  449.3 0.6 fusion.85
  449.9 0.1 dynamic_slice.50
  450.0 0.3 convolution_add_fusion.8
  450.4 0.3 fusion.44
  450.7 82.6 %psum.7 = f32[1,2,32,128]{3,2,1,0:T(8,128)} all-reduce(f32[1,2,32,128]{3,2,1,0:T(8,128)S(1)} %fusion.44), channel_id=1, replica_groups=mesh['row'=32,'col'=16] {'col'}, use_global_device_ids=true, to_apply=%region_8.10 | all-reduce | flops 8192 | bytes 65536 | tf_op jit(solution)/shard_map/psum | solution.py:99
  (30 shorter events, 0.3 us)
Async XLA Ops:
  7.2 0.9 copy-start
  7.2 79.4 %all-gather.8.cloned.1.call-start = ((), (), s32[]{:S(2)}) async-start(), calls=%async_computation.5 | async-start | bytes 1081344 | tf_op jit(solution)/shard_map/all_gather | solution.py:34
  9.7 189.1 %reduce-scatter.3.cloned.1.call-start = ((), (), s32[]{:S(2)}) async-start(), calls=%async_computation.2 | async-start | bytes 557056 | tf_op jit(solution)/shard_map/reduce_scatter | solution.py:49
  86.7 112.1 %copy-start.2 = (f32[1,1,2,32,128]{4,3,2,1,0:T(8,128)S(1)}, f32[1,1,2,32,128]{4,3,2,1,0:T(8,128)}, u32[]{:S(2)}) copy-start(f32[1,1,2,32,128]{4,3,2,1,0:T(8,128)} %param.20) | copy-start | bytes 98308
  86.7 112.1 %copy-start.3 = (f32[2,32,128]{2,1,0:T(8,128)S(1)}, f32[2,32,128]{2,1,0:T(8,128)}, u32[]{:S(2)}) copy-start(f32[2,32,128]{2,1,0:T(8,128)} %convolution_multiply_fusion.1) | copy-start | bytes 98308
  105.8 163.4 %copy-start.4 = (s32[32]{0:T(128)S(1)}, s32[32]{0:T(128)}, u32[]{:S(2)}) copy-start(s32[32]{0:T(128)} %get-tuple-element.489) | copy-start | bytes 388
  105.9 163.4 %copy-start.8 = (s32[32]{0:T(128)S(1)}, s32[32]{0:T(128)}, u32[]{:S(2)}) copy-start(s32[32]{0:T(128)} %get-tuple-element.491) | copy-start | bytes 388
  107.0 162.2 %all-gather.10.cloned.1.call-start = ((), (), s32[]{:S(2)}) async-start(), calls=%async_computation.6 | async-start | bytes 1081344 | tf_op jit(solution)/shard_map/all_gather | solution.py:34
  200.4 175.8 %reduce-scatter.5.cloned.1.call-start = ((), (), s32[]{:S(2)}) async-start(), calls=%async_computation.3 | async-start | bytes 557056 | tf_op jit(solution)/shard_map/reduce_scatter | solution.py:49
  269.3 109.0 %copy-start.6 = (f32[1,1,2,128]{3,2,1,0:T(2,128)S(1)}, f32[1,1,2,128]{3,2,1,0:T(2,128)}, u32[]{:S(2)}) copy-start(f32[1,1,2,128]{3,2,1,0:T(2,128)} %param.30) | copy-start | bytes 3076
  269.3 177.4 %copy-start.1 = (f32[1,1,16,128,128]{4,3,2,1,0:T(8,128)S(1)}, f32[1,1,16,128,128]{4,3,2,1,0:T(8,128)}, u32[]{:S(2)}) copy-start(f32[1,1,16,128,128]{4,3,2,1,0:T(8,128)} %param.26) | copy-start | bytes 3145732
  269.3 177.4 %copy-start.5 = (s32[1,1,16]{2,1,0:T(1,128)S(1)}, s32[1,1,16]{2,1,0:T(1,128)}, u32[]{:S(2)}) copy-start(s32[1,1,16]{2,1,0:T(1,128)} %param.28) | copy-start | bytes 196
  269.3 177.4 %copy-start.9 = (s32[1,1,16]{2,1,0:T(1,128)S(1)}, s32[1,1,16]{2,1,0:T(1,128)}, u32[]{:S(2)}) copy-start(s32[1,1,16]{2,1,0:T(1,128)} %param.27) | copy-start | bytes 196
  285.8 160.9 %all-gather.6.cloned.1.call-start = ((), (), s32[]{:S(2)}) async-start(), calls=%async_computation.4 | async-start | bytes 1081344 | tf_op jit(solution)/shard_map/all_gather | solution.py:34
  446.7 3.6 copy-start.7
Sparse Core Ops, SparseCore 0:
  11.7 74.8 all-gather.7
  107.1 91.6 reduce-scatter.2
  202.5 66.6 all-gather.9
  285.9 90.2 reduce-scatter.4
  379.8 66.8 all-gather.5
where the time goes:
time: 541 us; the launch traced here: 540 us
  waiting for transfers between devices  395 us (73%)
  blocking collectives  82.6 us (15%)
  matrix products  19.1 us (4%)
  local copies, waits for them, and re-layouts  18.2 us (3%)
  between operations  15.3 us (3%)
  other arithmetic  9.33 us (2%)
    all_gather x3, waiting for transfers between devices, gather_columns(): whole = lax.all_gather(vec[None, None], 'row', axis=0, tiled=True)  212 us
    reduce_scatter x2, waiting for transfers between devices, stiffness_product(): lax.psum_scatter(partial_value, 'col', scatter_dimension=1, tiled=True)  182 us
    psum x1, blocking collectives, body(): coarse = lax.psum(part, 'col')  82.6 us
    gather x7, local copies, waits for them, and re-layouts, add_group(): inputs = jnp.take(blocks, col_ids, axis=0)  12.5 us
  transfers between devices with their start and end apart: 5, of which 5 were waited for; matrix products, arithmetic and copies ran while one was open for 0% of the time, Pallas kernels for 0%

commit v1 on v0

--- a/solution.py
+++ b/solution.py
@@ -96,7 +96,7 @@
     ).astype(jnp.float32)
     tentative = jnp.dot(weighted, onehot, precision=highest)
     part = part + tentative.reshape(nrhs, pblocks, width).transpose(1, 0, 2)
-    coarse = lax.psum(part, "col")
+    coarse = jnp.sum(lax.all_gather(part, "col"), axis=0)
     return (relaxed_iterate[None, None], residual[None, None], coarse[None])
 
 

time: 541 us -> 507 us (0.937)
  blocking collectives: 82.6 us -> 47.6 us
    psum x1 -> x0, blocking collectives: 82.6 us -> none  [body(): coarse = lax.psum(part, 'col')]
    all_gather x0 -> x1, blocking collectives: none -> 47.6 us  [body(): coarse = jnp.sum(lax.all_gather(part, 'col'), axis=0)]
where the time goes in v1:
time: 507 us; the launch traced here: 505 us
  waiting for transfers between devices  395 us (78%)
  blocking collectives  47.6 us (9%)
  matrix products  19.1 us (4%)
  local copies, waits for them, and re-layouts  18.2 us (4%)
  between operations  15.3 us (3%)
  other arithmetic  9.98 us (2%)
    all_gather x3, waiting for transfers between devices, gather_columns(): whole = lax.all_gather(vec[None, None], 'row', axis=0, tiled=True)  212 us
    reduce_scatter x2, waiting for transfers between devices, stiffness_product(): lax.psum_scatter(partial_value, 'col', scatter_dimension=1, tiled=True)  182 us
    all_gather x1, blocking collectives, body(): coarse = jnp.sum(lax.all_gather(part, 'col'), axis=0)  47.6 us
    gather x7, local copies, waits for them, and re-layouts, add_group(): inputs = jnp.take(blocks, col_ids, axis=0)  12.5 us
    dot_general x7, matrix products, add_group(): product = jnp.einsum('ska,sab->skb', inputs, piece, precision=highest)  10.5 us
  transfers between devices with their start and end apart: 5, of which 5 were waited for; matrix products, arithmetic and copies ran while one was open for 0% of the time, Pallas kernels for 0%

profile of v1, /device:TPU:8, one launch (start us, length us, event | category | flops | bytes accessed | tf_op | source)
XLA Modules:
  0.0 505.5 jit_solution(13876492053143470296)
XLA Ops:
  7.2 0.0 copy-start
  7.2 0.0 all-gather.9.cloned.1.call-start
  7.2 0.8 copy-done
  8.1 1.6 convolution_multiply_fusion.1
  9.7 0.0 all-gather.9.cloned.1.call-update
  9.7 0.0 reduce-scatter.3.cloned.1.call-start
  10.4 76.2 %all-gather.9.cloned.1.call-done = f32[64,32,128]{2,1,0:T(8,128)} async-done(((f32[2,32,128]{2,1,0:T(8,128)}), f32[64,32,128]{2,1,0:T(8,128)}) %all-gather.9.cloned.1.call-update) | async-done | bytes 1048592 | tf_op jit(solution)/shard_map/all_gather | solution.py:34
  86.7 19.1 %while.30 = (s32[]{:T(128)}, f32[32,32,128]{2,0,1:T(8,128)S(1)}, s32[]{:T(128)}, s32[32]{0:T(128)}, s32[]{:T(128)}, /*index=5*/s32[32]{0:T(128)}, f32[64,32,128]...) while((s32[]{:T(128)}, f32[32,32,128]{2,0,1:T(8,128)S(1)}, ...), condition=%wide.region_1.3_spmd, body=%wide.region_0.2_spmd.sunk | while | flops 63080028 | bytes 2232807 | solution.py:30
  86.7 1.4 compare_and_fusion.6
  88.1 1.8 gather_fusion
  89.9 1.7 fusion.74
  91.6 0.7 dynamic_slice.46
  92.3 0.8 convolution_add_fusion.6
  93.1 1.4 compare_and_fusion.6
  94.5 1.8 gather_fusion
  96.3 1.7 fusion.74
  97.9 0.7 dynamic_slice.46
  98.7 0.8 convolution_add_fusion.6
  99.5 1.4 compare_and_fusion.6
  100.9 1.8 gather_fusion
  102.7 1.7 fusion.74
  104.3 0.7 dynamic_slice.46
  105.0 0.8 convolution_add_fusion.6
  105.9 1.1 copy.25
  107.0 0.0 reduce-scatter.3.cloned.1.call-update
  107.0 0.0 all-gather.11.cloned.1.call-start
  107.1 91.7 %reduce-scatter.3.cloned.1.call-done = f32[1,1,2,32,128]{4,3,2,1,0:T(8,128)} async-done(((f32[1,16,2,32,128]{4,3,2,1,0:T(8,128)}), f32[1,1,2,32,128]{4,3,2,1,0:T(8,128)}) %reduce-scatter.3.cloned.1.call-update) | async-done | bytes 32784 | tf_op jit(solution)/shard_map/reduce_scatter | solution.py:49
  198.8 1.6 fusion.44
  200.4 0.0 all-gather.11.cloned.1.call-update
  200.4 0.0 reduce-scatter.5.cloned.1.call-start
  200.5 68.7 %all-gather.11.cloned.1.call-done = f32[64,32,128]{2,1,0:T(8,128)} async-done(((f32[2,32,128]{2,1,0:T(8,128)}), f32[64,32,128]{2,1,0:T(8,128)}) %all-gather.11.cloned.1.call-update) | async-done | bytes 1048592 | tf_op jit(solution)/shard_map/all_gather | solution.py:34
  269.3 15.3 %while.31 = (s32[]{:T(128)}, f32[32,32,128]{2,0,1:T(8,128)S(1)}, s32[]{:T(128)}, s32[32]{0:T(128)S(1)}, s32[]{:T(128)}, /*index=5*/s32[32]{0:T(128)S(1)}, f32[64...) while((s32[]{:T(128)}, f32[32,32,128]{2,0,1:T(8,128)S(1)}, ...), condition=%wide.region_4.6_spmd, body=%wide.region_3.5_spmd.sunk | while | flops 63080028 | bytes 2232807 | solution.py:30
  269.3 0.8 compare_and_fusion.7
  270.2 1.8 gather_fusion.1
  271.9 1.7 fusion.79
  273.6 0.1 dynamic_slice.48
  273.7 0.8 convolution_add_fusion.7
  274.5 0.7 compare_and_fusion.7
  275.2 1.8 gather_fusion.1
  277.0 1.7 fusion.79
  278.7 0.1 dynamic_slice.48
  278.7 0.8 convolution_add_fusion.7
  279.6 0.7 compare_and_fusion.7
  280.3 1.8 gather_fusion.1
  282.1 1.7 fusion.79
  283.7 0.1 dynamic_slice.48
  283.8 0.8 convolution_add_fusion.7
  284.6 1.1 copy.26
  285.7 0.0 reduce-scatter.5.cloned.1.call-update
  285.8 0.0 all-gather.7.cloned.1.call-start
  285.8 90.4 %reduce-scatter.5.cloned.1.call-done = f32[1,1,2,32,128]{4,3,2,1,0:T(8,128)} async-done(((f32[1,16,2,32,128]{4,3,2,1,0:T(8,128)}), f32[1,1,2,32,128]{4,3,2,1,0:T(8,128)}) %reduce-scatter.5.cloned.1.call-update) | async-done | bytes 32784 | tf_op jit(solution)/shard_map/reduce_scatter | solution.py:49
  376.2 1.4 sub.30
  377.6 0.0 all-gather.7.cloned.1.call-update
  378.3 0.8 fusion.51
  379.2 67.5 %all-gather.7.cloned.1.call-done = f32[32,1,2,32,128]{4,3,2,1,0:T(8,128)} async-done(((f32[1,1,2,32,128]{4,3,2,1,0:T(8,128)}), f32[32,1,2,32,128]{4,3,2,1,0:T(8,128)}) %all-gather.7.cloned.1.call-update) | async-done | bytes 1048592 | tf_op jit(solution)/shard_map/all_gather | solution.py:34
  446.8 3.6 while.32
  446.8 0.7 compare_and_fusion.8
  447.5 1.8 gather_fusion.2
  449.3 0.6 fusion.84
  449.9 0.1 dynamic_slice.50
  450.0 0.3 convolution_add_fusion.8
  450.4 0.3 fusion.43
  450.7 47.6 %all-gather.2 = f32[32,32,128]{2,1,0:T(8,128)S(1)} all-gather(f32[2,32,128]{2,1,0:T(8,128)S(1)} %fusion.43), channel_id=4, replica_groups=mesh['row'=32,'col'=16] {'col'}, dimensions={0}, use_global_device_ids=true | all-gather | bytes 557056 | tf_op jit(solution)/shard_map/all_gather | solution.py:99
  498.3 0.6 reduce_sum.9
  (31 shorter events, 0.3 us)
Async XLA Ops:
  7.2 0.9 copy-start
  7.2 79.4 %all-gather.9.cloned.1.call-start = ((), (), s32[]{:S(2)}) async-start(), calls=%async_computation.5 | async-start | bytes 1081344 | tf_op jit(solution)/shard_map/all_gather | solution.py:34
  9.7 189.1 %reduce-scatter.3.cloned.1.call-start = ((), (), s32[]{:S(2)}) async-start(), calls=%async_computation.2 | async-start | bytes 557056 | tf_op jit(solution)/shard_map/reduce_scatter | solution.py:49
  86.7 112.1 %copy-start.2 = (f32[1,1,2,32,128]{4,3,2,1,0:T(8,128)S(1)}, f32[1,1,2,32,128]{4,3,2,1,0:T(8,128)}, u32[]{:S(2)}) copy-start(f32[1,1,2,32,128]{4,3,2,1,0:T(8,128)} %param.20) | copy-start | bytes 98308
  86.7 112.1 %copy-start.3 = (f32[2,32,128]{2,1,0:T(8,128)S(1)}, f32[2,32,128]{2,1,0:T(8,128)}, u32[]{:S(2)}) copy-start(f32[2,32,128]{2,1,0:T(8,128)} %convolution_multiply_fusion.1) | copy-start | bytes 98308
  105.8 163.4 %copy-start.4 = (s32[32]{0:T(128)S(1)}, s32[32]{0:T(128)}, u32[]{:S(2)}) copy-start(s32[32]{0:T(128)} %get-tuple-element.489) | copy-start | bytes 388
  105.9 163.4 %copy-start.8 = (s32[32]{0:T(128)S(1)}, s32[32]{0:T(128)}, u32[]{:S(2)}) copy-start(s32[32]{0:T(128)} %get-tuple-element.491) | copy-start | bytes 388
  107.0 162.2 %all-gather.11.cloned.1.call-start = ((), (), s32[]{:S(2)}) async-start(), calls=%async_computation.6 | async-start | bytes 1081344 | tf_op jit(solution)/shard_map/all_gather | solution.py:34
  200.4 175.8 %reduce-scatter.5.cloned.1.call-start = ((), (), s32[]{:S(2)}) async-start(), calls=%async_computation.3 | async-start | bytes 557056 | tf_op jit(solution)/shard_map/reduce_scatter | solution.py:49
  269.3 109.0 %copy-start.6 = (f32[1,1,2,128]{3,2,1,0:T(2,128)S(1)}, f32[1,1,2,128]{3,2,1,0:T(2,128)}, u32[]{:S(2)}) copy-start(f32[1,1,2,128]{3,2,1,0:T(2,128)} %param.30) | copy-start | bytes 3076
  269.3 177.4 %copy-start.1 = (f32[1,1,16,128,128]{4,3,2,1,0:T(8,128)S(1)}, f32[1,1,16,128,128]{4,3,2,1,0:T(8,128)}, u32[]{:S(2)}) copy-start(f32[1,1,16,128,128]{4,3,2,1,0:T(8,128)} %param.26) | copy-start | bytes 3145732
  269.3 177.4 %copy-start.5 = (s32[1,1,16]{2,1,0:T(1,128)S(1)}, s32[1,1,16]{2,1,0:T(1,128)}, u32[]{:S(2)}) copy-start(s32[1,1,16]{2,1,0:T(1,128)} %param.28) | copy-start | bytes 196
  269.3 177.4 %copy-start.9 = (s32[1,1,16]{2,1,0:T(1,128)S(1)}, s32[1,1,16]{2,1,0:T(1,128)}, u32[]{:S(2)}) copy-start(s32[1,1,16]{2,1,0:T(1,128)} %param.27) | copy-start | bytes 196
  285.8 160.9 %all-gather.7.cloned.1.call-start = ((), (), s32[]{:S(2)}) async-start(), calls=%async_computation.4 | async-start | bytes 1081344 | tf_op jit(solution)/shard_map/all_gather | solution.py:34
  446.7 3.6 copy-start.7
Sparse Core Ops, SparseCore 0:
  11.7 74.8 all-gather.8
  107.1 91.6 reduce-scatter.2
  202.5 66.6 all-gather.10
  285.9 90.2 reduce-scatter.4
  379.8 66.8 all-gather.6
